TPU v7x, 32 devices: a whole 2x2x4 slice. The times are simulated.
32 devices in a mesh: dp: 16 (over z, y, x), fsdp: 2 (over core).
Axes of the slice: x: 2, y: 2, z: 4, core: 2. Of those that a mesh axis runs over, the one named last changes fastest.
Arguments:
- tokens: bfloat16 [32, 256, 1152], P(('dp', 'fsdp')), may hold values from -6 to 6
- condition: bfloat16 [32, 1152], P(('dp', 'fsdp')), may hold values from -6 to 6
- cotangent: bfloat16 [32, 256, 1152], P(('dp', 'fsdp')), may hold values from -6 to 6
- image_grids: int32 [32, 2], P(('dp', 'fsdp')), may hold values from 12 to 20, as said below
- noise_bins: int32 [32], P(('dp', 'fsdp')), may hold values from 0 to 15, as said below
- bin_weights: int32 [16], replicated, may hold values from 1 to 4
- w_qkv: bfloat16 [1152, 3456], P('dp', 'fsdp'), may hold values from -0.1875 to 0.1875
- b_query: float32 [1152], replicated, may hold values from -3 to 3
- b_value: float32 [1152], replicated, may hold values from -0.625 to 0.625
- w_proj: bfloat16 [1152, 1152], P('dp', 'fsdp'), may hold values from -1.5 to 1.5
- b_proj: float32 [1152], replicated, may hold values from -1.75 to 1.75
- w_fc1: bfloat16 [1152, 4608], P('dp', 'fsdp'), may hold values from -0.1875 to 0.1875
- b_fc1: float32 [4608], replicated, may hold values from -3 to 3
- w_fc2: bfloat16 [4608, 1152], P('dp', 'fsdp'), may hold values from -0.09375 to 0.09375
- b_fc2: float32 [1152], replicated, may hold values from -1.75 to 1.75
- w_ada: bfloat16 [6912, 1152], replicated, may hold values from -0.1875 to 0.1875
- b_ada: float32 [6912], replicated, may hold values from -1.75 to 1.75
Outputs:
- result: bfloat16 [32, 256, 1152], P(('dp', 'fsdp'))
- grad_tokens: bfloat16 [32, 256, 1152], P(('dp', 'fsdp'))
- grad_condition: float32 [32, 1152], P(('dp', 'fsdp'))
- grad_w_qkv: float32 [1152, 3456], P('dp', 'fsdp')
- grad_b_query: float32 [1152], replicated
- grad_b_value: float32 [1152], replicated
- grad_w_proj: float32 [1152, 1152], P('dp', 'fsdp')
- grad_b_proj: float32 [1152], replicated
- grad_w_fc1: float32 [1152, 4608], P('dp', 'fsdp')
- grad_b_fc1: float32 [4608], replicated
- grad_w_fc2: float32 [4608, 1152], P('dp', 'fsdp')
- grad_b_fc2: float32 [1152], replicated
- grad_w_ada: float32 [6912, 1152], P(('dp', 'fsdp'))
- grad_b_ada: float32 [6912], replicated
Inputs may be any that keep to these rules, and one draw needn't show every extreme that they name: `image_grids`: each row is a height and a width that sum to 32; an image's tokens are the first height * width of its 256 slots. `noise_bins`: bin ids never fall along the image slots, and every bin holds at least one image.
All inputs are finite; a program needn't handle non-finite values.
Results may differ from a plain program's by a relative error of at most 0.014.
The roundings to bfloat16 on the way count: a program that leaves them out, or rounds other values in their place, can miss the bound.
Values may be sent and summed in bfloat16 or wider, within the bound.
A program may use at most 256 MiB of HBM per device.

v0:
```python
import jax
import jax.numpy as jnp
from jax import lax
from jax.sharding import PartitionSpec as P

D = 1152
H = 16
HD = 72
BINS = 16
SEQ = 256
NEG_FILL = -1e30
NORM_EPS = 1e-06
GELU_COEF = 0.7978845608028654
CUBIC_COEF = 0.044715
ROWS_DIMS = (((0,), (0,)), ((), ()))
LAST_DIMS = (((1,), (1,)), ((), ()))


def gelu_tanh(values_in):
    return (
        0.5
        * values_in
        * (1.0 + jnp.tanh(GELU_COEF * (values_in + CUBIC_COEF * values_in * values_in * values_in)))
    )


def norm_rows(inputs):
    centered = inputs - jnp.mean(inputs, axis=-1, keepdims=True)
    inverse = lax.rsqrt(jnp.mean(centered * centered, axis=-1, keepdims=True) + NORM_EPS)
    return (centered * inverse, inverse)


def norm_back(grad_normed, normed, inverse):
    centered_grad = grad_normed - jnp.mean(grad_normed, axis=-1, keepdims=True)
    return inverse * (
        centered_grad - normed * jnp.mean(grad_normed * normed, axis=-1, keepdims=True)
    )


def collect_trunk(w_qkv, w_proj, w_fc1, w_fc2):
    paired = (
        lax.all_gather(w_qkv, "fsdp", axis=1, tiled=True),
        lax.all_gather(w_proj, "fsdp", axis=1, tiled=True),
        lax.all_gather(w_fc1, "fsdp", axis=1, tiled=True),
        lax.all_gather(w_fc2, "fsdp", axis=1, tiled=True),
    )
    return (
        lax.all_gather(paired[0], "dp", axis=0, tiled=True),
        lax.all_gather(paired[1], "dp", axis=0, tiled=True),
        lax.all_gather(paired[2], "dp", axis=0, tiled=True),
        lax.all_gather(paired[3], "dp", axis=0, tiled=True),
    )


def masked_scores(query, keys, valid_keys):
    scaled = jnp.einsum(
        "blhc,bmhc->bhlm", query, keys, preferred_element_type=jnp.float32
    ) * HD ** (-0.5)
    return jnp.where(valid_keys[:, None, None, :], scaled, NEG_FILL)


def shards(
    tokens,
    condition,
    cotangent,
    image_grids,
    noise_bins,
    bin_weights,
    w_qkv,
    b_query,
    b_value,
    w_proj,
    b_proj,
    w_fc1,
    b_fc1,
    w_fc2,
    b_fc2,
    w_ada,
    b_ada,
):
    images = tokens.shape[0]
    row_count = images * SEQ
    token_count = image_grids[:, 0] * image_grids[:, 1]
    valid_keys = lax.broadcasted_iota(jnp.int32, (images, SEQ), 1) < token_count[:, None]
    bin_table = (noise_bins[:, None] == lax.broadcasted_iota(jnp.int32, (images, BINS), 1)).astype(
        jnp.float32
    )
    local_counts = jnp.sum(bin_table * token_count[:, None].astype(jnp.float32), axis=0)
    counts = lax.psum(local_counts, ("dp", "fsdp"))
    bin_scale = bin_weights.astype(jnp.float32) * (jnp.sum(counts) / BINS) / counts
    image_scale = jnp.sum(bin_table * bin_scale[None, :], axis=1)
    full_qkv, full_proj, full_fc1, full_fc2 = collect_trunk(w_qkv, w_proj, w_fc1, w_fc2)
    cond_float = condition.astype(jnp.float32)
    silu_cond = jax.nn.silu(cond_float).astype(jnp.bfloat16)
    modul = lax.dot_general(silu_cond, w_ada, LAST_DIMS, preferred_element_type=jnp.float32) + b_ada
    pieces = [modul[:, None, part_index * D : (part_index + 1) * D] for part_index in range(6)]
    shift_one, scale_one, gate_one, shift_two, scale_two, gate_two = pieces
    token_float = tokens.astype(jnp.float32)
    normed_one, inverse_one = norm_rows(token_float)
    attn_in = (
        (normed_one * (1.0 + scale_one) + shift_one).astype(jnp.bfloat16).reshape(row_count, D)
    )
    bias_qkv = jnp.concatenate([b_query, jnp.zeros_like(b_query), b_value])
    qkv_all = (jnp.dot(attn_in, full_qkv, preferred_element_type=jnp.float32) + bias_qkv).astype(
        jnp.bfloat16
    )
    qkv_heads = qkv_all.reshape(images, SEQ, 3, H, HD)
    query, keys, values = (qkv_heads[:, :, 0], qkv_heads[:, :, 1], qkv_heads[:, :, 2])
    scores = masked_scores(query, keys, valid_keys)
    row_max = jnp.max(scores, axis=-1, keepdims=True)
    exponent = jnp.exp(scores - row_max)
    row_total = jnp.sum(exponent, axis=-1, keepdims=True)
    soft_probs = exponent / row_total
    log_total = row_max + jnp.log(row_total)
    attended = jnp.einsum(
        "bhlm,bmhc->blhc",
        soft_probs.astype(jnp.bfloat16),
        values,
        preferred_element_type=jnp.float32,
    )
    attended = attended.astype(jnp.bfloat16).reshape(row_count, D)
    attn_out = (jnp.dot(attended, full_proj, preferred_element_type=jnp.float32) + b_proj).reshape(
        images, SEQ, D
    )
    middle = token_float + gate_one * attn_out
    normed_two, inverse_two = norm_rows(middle)
    mlp_in = (normed_two * (1.0 + scale_two) + shift_two).astype(jnp.bfloat16).reshape(row_count, D)
    hidden = jnp.dot(mlp_in, full_fc1, preferred_element_type=jnp.float32) + b_fc1
    active = gelu_tanh(hidden).astype(jnp.bfloat16)
    branch = (jnp.dot(active, full_fc2, preferred_element_type=jnp.float32) + b_fc2).reshape(
        images, SEQ, D
    )
    result = (middle + gate_two * branch).astype(jnp.bfloat16)
    back_qkv, back_proj, back_fc1, back_fc2 = (full_qkv, full_proj, full_fc1, full_fc2)
    grad_out = (
        cotangent.astype(jnp.float32)
        * (valid_keys.astype(jnp.float32) * image_scale[:, None])[:, :, None]
    )
    d_gate_two = jnp.sum(grad_out * branch, axis=1)
    d_branch = (gate_two * grad_out).astype(jnp.bfloat16).reshape(row_count, D)
    grad_fc2 = lax.dot_general(active, d_branch, ROWS_DIMS, preferred_element_type=jnp.float32)
    bias_fc2 = jnp.sum(d_branch, axis=0, dtype=jnp.float32)
    d_active = lax.dot_general(d_branch, back_fc2, LAST_DIMS, preferred_element_type=jnp.float32)
    gelu_pull = jax.vjp(gelu_tanh, hidden)[1]
    d_hidden = gelu_pull(d_active)[0].astype(jnp.bfloat16)
    grad_fc1 = lax.dot_general(mlp_in, d_hidden, ROWS_DIMS, preferred_element_type=jnp.float32)
    bias_fc1 = jnp.sum(d_hidden, axis=0, dtype=jnp.float32)
    d_mlp_in = lax.dot_general(
        d_hidden, back_fc1, LAST_DIMS, preferred_element_type=jnp.float32
    ).reshape(images, SEQ, D)
    d_shift_two = jnp.sum(d_mlp_in, axis=1)
    d_scale_two = jnp.sum(d_mlp_in * normed_two, axis=1)
    d_middle = grad_out + norm_back(d_mlp_in * (1.0 + scale_two), normed_two, inverse_two)
    d_gate_one = jnp.sum(d_middle * attn_out, axis=1)
    d_attn = (gate_one * d_middle).astype(jnp.bfloat16).reshape(row_count, D)
    grad_proj = lax.dot_general(attended, d_attn, ROWS_DIMS, preferred_element_type=jnp.float32)
    bias_proj = jnp.sum(d_attn, axis=0, dtype=jnp.float32)
    d_attended = lax.dot_general(d_attn, back_proj, LAST_DIMS, preferred_element_type=jnp.float32)
    d_attended = d_attended.astype(jnp.bfloat16).reshape(images, SEQ, H, HD)
    soft_again = jnp.exp(masked_scores(query, keys, valid_keys) - log_total)
    grad_values = jnp.einsum(
        "bhlm,blhc->bmhc",
        soft_again.astype(jnp.bfloat16),
        d_attended,
        preferred_element_type=jnp.float32,
    )
    d_probs = jnp.einsum("blhc,bmhc->bhlm", d_attended, values, preferred_element_type=jnp.float32)
    d_scores = soft_again * (d_probs - jnp.sum(soft_again * d_probs, axis=-1, keepdims=True))
    d_scores = jnp.where(valid_keys[:, None, None, :], d_scores, 0.0).astype(jnp.bfloat16)
    grad_query = jnp.einsum(
        "bhlm,bmhc->blhc", d_scores, keys, preferred_element_type=jnp.float32
    ) * HD ** (-0.5)
    grad_keys = jnp.einsum(
        "bhlm,blhc->bmhc", d_scores, query, preferred_element_type=jnp.float32
    ) * HD ** (-0.5)
    d_qkv = (
        jnp.stack([grad_query, grad_keys, grad_values], axis=2)
        .astype(jnp.bfloat16)
        .reshape(row_count, 3 * D)
    )
    grad_qkv = lax.dot_general(attn_in, d_qkv, ROWS_DIMS, preferred_element_type=jnp.float32)
    bias_query = jnp.sum(d_qkv[:, :D], axis=0, dtype=jnp.float32)
    bias_value = jnp.sum(d_qkv[:, 2 * D :], axis=0, dtype=jnp.float32)
    d_attn_in = lax.dot_general(
        d_qkv, back_qkv, LAST_DIMS, preferred_element_type=jnp.float32
    ).reshape(images, SEQ, D)
    d_shift_one = jnp.sum(d_attn_in, axis=1)
    d_scale_one = jnp.sum(d_attn_in * normed_one, axis=1)
    grad_tokens = (
        d_middle + norm_back(d_attn_in * (1.0 + scale_one), normed_one, inverse_one)
    ).astype(jnp.bfloat16)
    d_modul = jnp.concatenate(
        [d_shift_one, d_scale_one, d_gate_one, d_shift_two, d_scale_two, d_gate_two], axis=1
    ).astype(jnp.bfloat16)
    silu_pull = jax.vjp(jax.nn.silu, cond_float)[1]
    grad_condition = silu_pull(jnp.dot(d_modul, w_ada, preferred_element_type=jnp.float32))[0]
    bias_ada = jnp.sum(d_modul, axis=0, dtype=jnp.float32)
    spread_dp = (
        lax.psum_scatter(grad_qkv, "dp", scatter_dimension=0, tiled=True),
        lax.psum_scatter(grad_proj, "dp", scatter_dimension=0, tiled=True),
        lax.psum_scatter(grad_fc1, "dp", scatter_dimension=0, tiled=True),
        lax.psum_scatter(grad_fc2, "dp", scatter_dimension=0, tiled=True),
    )
    owned = (
        lax.psum_scatter(
            spread_dp[0].astype(jnp.bfloat16), "fsdp", scatter_dimension=1, tiled=True
        ).astype(jnp.float32),
        lax.psum_scatter(
            spread_dp[1].astype(jnp.bfloat16), "fsdp", scatter_dimension=1, tiled=True
        ).astype(jnp.float32),
        lax.psum_scatter(
            spread_dp[2].astype(jnp.bfloat16), "fsdp", scatter_dimension=1, tiled=True
        ).astype(jnp.float32),
        lax.psum_scatter(
            spread_dp[3].astype(jnp.bfloat16), "fsdp", scatter_dimension=1, tiled=True
        ).astype(jnp.float32),
    )
    summed_bias = lax.psum(
        (bias_query, bias_value, bias_proj, bias_fc1, bias_fc2, bias_ada), ("dp", "fsdp")
    )
    share_rows = 6 * D // lax.axis_size(("dp", "fsdp"))
    own_start = lax.axis_index(("dp", "fsdp")) * share_rows
    columns = lax.dynamic_slice_in_dim(
        lax.all_gather(d_modul, ("dp", "fsdp"), axis=0, tiled=True), own_start, share_rows, 1
    )
    grad_ada = lax.dot_general(
        columns,
        lax.all_gather(silu_cond, ("dp", "fsdp"), axis=0, tiled=True),
        ROWS_DIMS,
        preferred_element_type=jnp.float32,
    )
    return (
        result,
        grad_tokens,
        grad_condition,
        owned[0],
        summed_bias[0],
        summed_bias[1],
        owned[1],
        summed_bias[2],
        owned[2],
        summed_bias[3],
        owned[3],
        summed_bias[4],
        grad_ada,
        summed_bias[5],
    )


def solution(mesh):
    in_specs = (
        P(("dp", "fsdp"), None, None),
        P(("dp", "fsdp"), None),
        P(("dp", "fsdp"), None, None),
        P(("dp", "fsdp"), None),
        P(("dp", "fsdp")),
        P(),
        P("dp", "fsdp"),
        P(),
        P(),
        P("dp", "fsdp"),
        P(),
        P("dp", "fsdp"),
        P(),
        P("dp", "fsdp"),
        P(),
        P(),
        P(),
    )
    out_specs = (
        P(("dp", "fsdp"), None, None),
        P(("dp", "fsdp"), None, None),
        P(("dp", "fsdp"), None),
        P("dp", "fsdp"),
        P(),
        P(),
        P("dp", "fsdp"),
        P(),
        P("dp", "fsdp"),
        P(),
        P("dp", "fsdp"),
        P(),
        P(("dp", "fsdp"), None),
        P(),
    )
    return jax.shard_map(shards, mesh=mesh, in_specs=in_specs, out_specs=out_specs, check_vma=False)
```

profile of v0, /device:TPU:0, one launch (start us, length us, event | category | flops | bytes accessed | tf_op | source)
XLA Modules:
  0.0 1598.3 jit_solution(9398244737780951491)
XLA Ops:
  7.2 2.6 all-gather
  24.0 44.7 %psum.49 = f32[16]{0:T(128)S(1)} all-reduce(f32[16]{0:T(128)S(1)} %compare_select_fusion.1), channel_id=1, replica_groups=mesh['dp'=16,'fsdp'=2] {'dp','fsdp'}, use_global_device_ids=true, to_apply=%region_6.7 | all-reduce | flops 16 | bytes 128 | tf_op jit(solution)/shard_map/psum | solution.py:89
  69.3 10.2 convolution_reduce_fusion
  83.8 39.2 %all-gather.10.cloned.1.call-done = bf16[1152,3456]{1,0:T(8,128)(2,1)} async-done(((bf16[72,3456]{1,0:T(8,128)(2,1)}), bf16[1152,3456]{1,0:T(8,128)(2,1)}) %all-gather.10.cloned.1.call-update) | async-done | bytes 7962640 | tf_op jit(solution)/shard_map/all_gather | solution.py:48
  123.0 7.2 fusion.1
  137.6 51.1 %all-gather.12.cloned.1.call-done = bf16[1152,1152]{1,0:T(8,128)(2,1)} async-done(((bf16[72,1152]{1,0:T(8,128)(2,1)}), bf16[1152,1152]{1,0:T(8,128)(2,1)}) %all-gather.12.cloned.1.call-update) | async-done | bytes 2654224 | tf_op jit(solution)/shard_map/all_gather | solution.py:49
  188.7 4.1 fusion.102
  194.2 128.6 %all-gather.14.cloned.1.call-done = bf16[1152,4608]{1,0:T(8,128)(2,1)} async-done(((bf16[72,4608]{1,0:T(8,128)(2,1)}), bf16[1152,4608]{1,0:T(8,128)(2,1)}) %all-gather.14.cloned.1.call-update) | async-done | bytes 10616848 | tf_op jit(solution)/shard_map/all_gather | solution.py:50
  322.8 9.0 convolution_add_fusion
  331.8 125.2 %all-gather.16.cloned.1.call-done = bf16[4608,1152]{1,0:T(8,128)(2,1)} async-done(((bf16[288,1152]{1,0:T(8,128)(2,1)}), bf16[4608,1152]{1,0:T(8,128)(2,1)}) %all-gather.16.cloned.1.call-update) | async-done | bytes 10616848 | tf_op jit(solution)/shard_map/all_gather | solution.py:51
  457.0 10.2 convert_reduce_fusion
  467.2 8.8 fusion.98
  476.1 9.3 fusion.62
  488.5 3.2 fusion.105
  493.4 3.8 convolution_convert_fusion
  499.4 3.8 fusion.73
  503.2 8.6 fusion.43
  511.8 8.6 fusion.49
  520.5 3.2 fusion.37
  524.4 8.1 fusion.86
  533.0 14.1 fusion.89
  547.2 12.1 fusion.95
  560.0 41.9 %all-gather.4 = bf16[32,1,1152]{2,1,0:T(2,128)(2,1)} all-gather(bf16[1,1,1152]{2,1,0:T(2,128)(2,1)S(1)} %copy-done.41), channel_id=1, replica_groups=mesh['dp'=16,'fsdp'=2] {'dp','fsdp'}, dimensions={0}, use_global_device_ids=true | all-gather | bytes 76032 | tf_op jit(solution)/shard_map/all_gather | solution.py:228
  601.9 30.4 %reduce-scatter.33.cloned.1.call-done = f32[72,1152]{1,0:T(8,128)} async-done(((f32[1152,1152]{1,0:T(8,128)}), f32[72,1152]{1,0:T(8,128)}) %reduce-scatter.33.cloned.1.call-update) | async-done | bytes 331792
  634.3 6.7 fusion.60
  642.8 246.3 %reduce-scatter.31.cloned.1.call-done = f32[72,3456]{1,0:T(8,128)} async-done(((f32[1152,3456]{1,0:T(8,128)}), f32[72,3456]{1,0:T(8,128)}) %reduce-scatter.31.cloned.1.call-update) | async-done | bytes 995344
  895.6 3.6 fusion.64
  899.2 307.8 %reduce-scatter.23.cloned.1.call-done = f32[288,1152]{1,0:T(8,128)} async-done(((f32[4608,1152]{1,0:T(8,128)}), f32[288,1152]{1,0:T(8,128)}) %reduce-scatter.23.cloned.1.call-update) | async-done | bytes 1327120 | tf_op jit(solution)/shard_map/reduce_scatter | solution.py:202
  1209.9 47.2 %all-gather.3 = bf16[32,1,6912]{2,1,0:T(2,128)(2,1)S(1)} all-gather(bf16[1,1,6912]{2,1,0:T(2,128)(2,1)S(1)} %bitcast.186), channel_id=1, replica_groups=mesh['dp'=16,'fsdp'=2] {'dp','fsdp'}, dimensions={0}, use_global_device_ids=true | all-gather | bytes 456192 | tf_op jit(solution)/shard_map/all_gather | solution.py:224
  1257.2 271.1 %reduce-scatter.19.cloned.1.call-done = f32[72,4608]{1,0:T(8,128)} async-done(((f32[1152,4608]{1,0:T(8,128)}), f32[72,4608]{1,0:T(8,128)}) %reduce-scatter.19.cloned.1.call-update) | async-done | bytes 1327120 | tf_op jit(solution)/shard_map/reduce_scatter | solution.py:201
  1532.6 41.1 %all-reduce.2 = (f32[1152]{0:T(1024)}, f32[1152]{0:T(1024)}, f32[1152]{0:T(1024)}, f32[4608]{0:T(1024)}, f32[1152]{0:T(1024)}, /*index=5*/f32[6912]{0:T(1024)}) all-reduce(f32[1152]{0:T(1024)S(1)} %get-tuple-element.19, f32[1152]{0:T(1024)S(1)} %get-tuple-element.18, ...), channel_id=1, replica_groups=mesh['dp'=16,'fsdp'=2] {'dp','fsdp'}, use_global_device_ids=true, to_apply=%region_23.24 | all-reduce | flops 16128 | bytes 115200 | tf_op jit(solution)/shard_map/psum | solution.py:218
  1575.2 8.3 fusion.78
  (205 shorter events, 60.5 us)
Async XLA Ops:
  7.2 115.8 %all-gather.10.cloned.1.call-start = ((), (), s32[]{:S(2)}) async-start(), calls=%async_computation.8 | async-start | bytes 8460288 | tf_op jit(solution)/shard_map/all_gather | solution.py:48
  11.5 177.2 %all-gather.12.cloned.1.call-start = ((), (), s32[]{:S(2)}) async-start(), calls=%async_computation.9 | async-start | bytes 2820096 | tf_op jit(solution)/shard_map/all_gather | solution.py:49
  14.5 308.3 %all-gather.14.cloned.1.call-start = ((), (), s32[]{:S(2)}) async-start(), calls=%async_computation.10 | async-start | bytes 11280384 | tf_op jit(solution)/shard_map/all_gather | solution.py:50
  17.0 440.0 %all-gather.16.cloned.1.call-start = ((), (), s32[]{:S(2)}) async-start(), calls=%async_computation.11 | async-start | bytes 11280384 | tf_op jit(solution)/shard_map/all_gather | solution.py:51
  17.1 51.5 %copy-start.22 = (bf16[1,1152]{1,0:T(2,128)(2,1)S(1)}, bf16[1,1152]{1,0:T(2,128)(2,1)}, u32[]{:S(2)}) copy-start(bf16[1,1152]{1,0:T(2,128)(2,1)} %param.18) | copy-start | bytes 6916
  21.3 610.9 %reduce-scatter.33.cloned.1.call-start = ((), (), s32[]{:S(2)}) async-start(), calls=%async_computation.19 | async-start | bytes 5640192
  80.8 52.1 %copy-start.50 = (pred[256]{0:T(512)(128)(4,1)}, pred[256]{0:T(512)(128)(4,1)S(1)}, u32[]{:S(2)}) copy-start(pred[256]{0:T(512)(128)(4,1)S(1)} %iota_compare_fusion) | copy-start | bytes 772
  83.3 39.7 %copy-start.15 = (f32[1152]{0:T(1024)}, f32[1152]{0:T(1024)S(1)}, u32[]{:S(2)}) copy-start(f32[1152]{0:T(1024)S(1)} %get-tuple-element.27) | copy-start | bytes 13828
  83.5 39.5 %copy-start.27 = (f32[256]{0:T(256)}, f32[256]{0:T(256)S(1)}, u32[]{:S(2)}) copy-start(f32[256]{0:T(256)S(1)} %broadcast_multiply_fusion.5) | copy-start | bytes 3076
  491.8 397.3 %reduce-scatter.31.cloned.1.call-start = ((), (), s32[]{:S(2)}) async-start(), calls=%async_computation.18 | async-start | bytes 16920576
  532.5 674.5 %reduce-scatter.23.cloned.1.call-start = ((), (), s32[]{:S(2)}) async-start(), calls=%async_computation.14 | async-start | bytes 22560768 | tf_op jit(solution)/shard_map/reduce_scatter | solution.py:202
  547.1 981.2 %reduce-scatter.19.cloned.1.call-start = ((), (), s32[]{:S(2)}) async-start(), calls=%async_computation.12 | async-start | bytes 22560768 | tf_op jit(solution)/shard_map/reduce_scatter | solution.py:201
  559.3 74.9 %copy-start.29 = (f32[256]{0:T(256)S(1)}, f32[256]{0:T(256)}, u32[]{:S(2)}) copy-start(f32[256]{0:T(256)} %copy-done.27) | copy-start | bytes 3076
  559.3 74.9 %copy-start.38 = (f32[256]{0:T(256)S(1)}, f32[256]{0:T(256)}, u32[]{:S(2)}) copy-start(f32[256]{0:T(256)} %copy-done.36) | copy-start | bytes 3076
  559.3 1024.1 %reduce-scatter.27.cloned.1.call-start = ((), (), s32[]{:S(2)}) async-start(), calls=%async_computation.16 | async-start | bytes 442368
  634.2 951.0 %reduce-scatter.25.cloned.1.call-start = ((), (), s32[]{:S(2)}) async-start(), calls=%async_computation.15 | async-start | bytes 1327104
  642.8 252.8 %copy-start.3 = (f32[256,1152]{1,0:T(8,128)S(1)}, f32[256,1152]{1,0:T(8,128)}, u32[]{:S(2)}) copy-start(f32[256,1152]{1,0:T(8,128)} %get-tuple-element.54) | copy-start | bytes 3538948
  893.4 693.8 %reduce-scatter.29.cloned.1.call-start = ((), (), s32[]{:S(2)}) async-start(), calls=%async_computation.17 | async-start | bytes 1327104
  899.2 310.6 %copy-start.26 = (bf16[1,6912]{1,0:T(2,128)(2,1)S(1)}, bf16[1,6912]{1,0:T(2,128)(2,1)}, u32[]{:S(2)}) copy-start(bf16[1,6912]{1,0:T(2,128)(2,1)} %constant_dynamic-update-slice_fusion.5) | copy-start | bytes 41476
  899.2 310.6 %copy-start.45 = (bf16[1152]{0:T(1024)(128)(2,1)S(1)}, bf16[1152]{0:T(1024)(128)(2,1)}, u32[]{:S(2)}) copy-start(bf16[1152]{0:T(1024)(128)(2,1)} %get-tuple-element.16) | copy-start | bytes 6916
  899.2 310.7 %copy-start.32 = (bf16[1152]{0:T(1024)(128)(2,1)S(1)}, bf16[1152]{0:T(1024)(128)(2,1)}, u32[]{:S(2)}) copy-start(bf16[1152]{0:T(1024)(128)(2,1)} %get-tuple-element.47) | copy-start | bytes 6916
  899.2 310.7 %copy-start.44 = (bf16[1152]{0:T(1024)(128)(2,1)S(1)}, bf16[1152]{0:T(1024)(128)(2,1)}, u32[]{:S(2)}) copy-start(bf16[1152]{0:T(1024)(128)(2,1)} %get-tuple-element.20) | copy-start | bytes 6916
  899.2 310.7 %copy-start.43 = (bf16[1152]{0:T(1024)(128)(2,1)S(1)}, bf16[1152]{0:T(1024)(128)(2,1)}, u32[]{:S(2)}) copy-start(bf16[1152]{0:T(1024)(128)(2,1)} %get-tuple-element.46) | copy-start | bytes 6916
  899.2 310.7 %copy-start.42 = (bf16[1152]{0:T(1024)(128)(2,1)S(1)}, bf16[1152]{0:T(1024)(128)(2,1)}, u32[]{:S(2)}) copy-start(bf16[1152]{0:T(1024)(128)(2,1)} %get-tuple-element.43) | copy-start | bytes 6916
  1209.7 379.6 %reduce-scatter.21.cloned.1.call-start = ((), (), s32[]{:S(2)}) async-start(), calls=%async_computation.13 | async-start | bytes 995328 | tf_op jit(solution)/shard_map/reduce_scatter | solution.py:211
  1257.2 273.8 %copy-start.21 = (bf16[6912]{0:T(1024)(128)(2,1)S(1)}, bf16[6912]{0:T(1024)(128)(2,1)}, u32[]{:S(2)}) copy-start(bf16[6912]{0:T(1024)(128)(2,1)} %custom-call.1) | copy-start | bytes 41476
  1257.2 275.4 %copy-start.33 = (f32[1152]{0:T(1024)S(1)}, f32[1152]{0:T(1024)}, u32[]{:S(2)}) copy-start(f32[1152]{0:T(1024)} %get-tuple-element.38) | copy-start | bytes 13828
  1257.2 275.4 %copy-start.34 = (f32[1152]{0:T(1024)S(1)}, f32[1152]{0:T(1024)}, u32[]{:S(2)}) copy-start(f32[1152]{0:T(1024)} %get-tuple-element.49) | copy-start | bytes 13828
  1257.2 275.4 %copy-start.40 = (f32[4608]{0:T(1024)S(1)}, f32[4608]{0:T(1024)}, u32[]{:S(2)}) copy-start(f32[4608]{0:T(1024)} %get-tuple-element.57) | copy-start | bytes 55300
  1257.2 316.7 %copy-start.12 = (bf16[32,1,1152]{2,1,0:T(2,128)(2,1)S(1)}, bf16[32,1,1152]{2,1,0:T(2,128)(2,1)}, u32[]{:S(2)}) copy-start(bf16[32,1,1152]{2,1,0:T(2,128)(2,1)} %all-gather.4) | copy-start | bytes 221188
  1530.5 44.6 %copy-start.23 = (bf16[1,1152]{1,0:T(2,128)(2,1)S(1)}, bf16[1,1152]{1,0:T(2,128)(2,1)}, u32[]{:S(2)}) copy-start(bf16[1,1152]{1,0:T(2,128)(2,1)} %param.18) | copy-start | bytes 6916
  1530.5 44.6 %copy-start.25 = (f32[1,1152]{1,0:T(1,128)S(1)}, f32[1,1152]{1,0:T(1,128)}, u32[]{:S(2)}) copy-start(f32[1,1152]{1,0:T(1,128)} %copy-done.24) | copy-start | bytes 13828
  (33 other events, 235.5 us)
Sparse Core Ops, SparseCore 0:
  11.6 111.3 all-gather.9
  126.2 62.4 all-gather.11
  191.5 131.2 all-gather.13
  326.0 130.9 all-gather.15
  491.9 140.3 reduce-scatter.32
  637.9 251.1 reduce-scatter.30
  895.1 311.8 reduce-scatter.22
  1213.0 315.2 reduce-scatter.18
  1531.1 6.8 reduce-scatter.26
  1540.2 9.3 reduce-scatter.24
  1551.8 9.3 reduce-scatter.28
  1564.0 9.2 reduce-scatter.20
where the time goes:
time: 1600 us
  waiting for transfers between devices  1200 us (75%)
  blocking collectives  184 us (12%)
  matrix products  143 us (9%)
  other arithmetic  26.5 us (2%)
  local copies, waits for them, and re-layouts  25.3 us (2%)
  between operations  17.6 us (1%)
    reduce_scatter x1, waiting for transfers between devices, shards(): lax.psum_scatter(grad_fc2, 'dp', scatter_dimension=0, tiled=True)  308 us
    unnamed x17, waiting for transfers between devices  277 us
    reduce_scatter x1, waiting for transfers between devices, shards(): lax.psum_scatter(grad_fc1, 'dp', scatter_dimension=0, tiled=True)  271 us
    all_gather x1, waiting for transfers between devices, collect_trunk(): lax.all_gather(paired[2], 'dp', axis=0, tiled=True)  129 us
    all_gather x1, waiting for transfers between devices, collect_trunk(): lax.all_gather(paired[3], 'dp', axis=0, tiled=True)  125 us
    all_gather x1, waiting for transfers between devices, collect_trunk(): lax.all_gather(paired[1], 'dp', axis=0, tiled=True)  51.1 us
    all_gather x1, blocking collectives, shards(): lax.all_gather(d_modul, ('dp', 'fsdp'), axis=0, tiled=True)  47.2 us
    psum x1, blocking collectives, shards(): counts = lax.psum(local_counts, ('dp', 'fsdp'))  44.7 us
  transfers between devices with their start and end apart: 12, of which 8 were waited for; matrix products, arithmetic and copies ran while one was open for 10% of the time, Pallas kernels for 0%

commit v1 on v0

--- a/solution.py
+++ b/solution.py
@@ -16,6 +16,29 @@
 LAST_DIMS = (((1,), (1,)), ((), ()))
 
 
+def _take_samples_all(own_rows, axis_tag):
+    piece_next, e_next, y_new = (
+        jax.lax.axis_size(axis_tag),
+        jax.lax.axis_index(axis_tag),
+        own_rows.shape[0],
+    )
+    frame_out, odd = (own_rows, 1)
+    while odd < piece_next:
+        frame_out = jnp.concatenate(
+            [
+                frame_out,
+                jax.lax.ppermute(
+                    frame_out,
+                    axis_tag,
+                    perm=tuple(((d, (d - odd) % piece_next) for d in range(piece_next))),
+                ),
+            ],
+            0,
+        )
+        odd = 2 * odd
+    return jnp.roll(frame_out, e_next * y_new, 0)
+
+
 def gelu_tanh(values_in):
     return (
         0.5
@@ -45,7 +68,7 @@
         lax.all_gather(w_fc2, "fsdp", axis=1, tiled=True),
     )
     return (
-        lax.all_gather(paired[0], "dp", axis=0, tiled=True),
+        _take_samples_all(paired[0], "dp"),
         lax.all_gather(paired[1], "dp", axis=0, tiled=True),
         lax.all_gather(paired[2], "dp", axis=0, tiled=True),
         lax.all_gather(paired[3], "dp", axis=0, tiled=True),

time: 1600 us -> 1710 us (1.069)
  blocking collectives: 184 us -> 358 us
  waiting for transfers between devices: 1200 us -> 1110 us
    psum x1, blocking collectives: 44.7 us -> 215 us  [shards(): counts = lax.psum(local_counts, ('dp', 'fsdp'))]
    ppermute x0 -> x4, waiting for transfers between devices: none -> 80.9 us  [_take_samples_all(): jax.lax.ppermute(frame_out, axis_tag, perm=tuple(((d, (d - odd) % piece_n...]
    all_gather x1, waiting for transfers between devices: 129 us -> 51.8 us  [collect_trunk(): lax.all_gather(paired[2], 'dp', axis=0, tiled=True)]
    all_gather x1, waiting for transfers between devices: 51.1 us -> 0.01 us  [collect_trunk(): lax.all_gather(paired[1], 'dp', axis=0, tiled=True)]
    all_gather x1 -> x0, waiting for transfers between devices: 39.2 us -> none  [collect_trunk(): lax.all_gather(paired[0], 'dp', axis=0, tiled=True)]
    unnamed x17 -> x16, waiting for transfers between devices: 277 us -> 275 us
  transfers between devices with their start and end apart: 12 -> 15, of which waited for: 8 -> 9; matrix products, arithmetic and copies ran while one was open for 10% -> 9% of each run, Pallas kernels for 0% -> 0%
where the time goes in v1:
time: 1710 us
  waiting for transfers between devices  1110 us (65%)
  blocking collectives  358 us (21%)
  matrix products  140 us (8%)
  local copies, waits for them, and re-layouts  38.4 us (2%)
  other arithmetic  29.5 us (2%)
  between operations  17.5 us (1%)
    reduce_scatter x1, waiting for transfers between devices, shards(): lax.psum_scatter(grad_fc2, 'dp', scatter_dimension=0, tiled=True)  308 us
    unnamed x16, waiting for transfers between devices  275 us
    reduce_scatter x1, waiting for transfers between devices, shards(): lax.psum_scatter(grad_fc1, 'dp', scatter_dimension=0, tiled=True)  272 us
    psum x1, blocking collectives, shards(): counts = lax.psum(local_counts, ('dp', 'fsdp'))  215 us
    all_gather x1, waiting for transfers between devices, collect_trunk(): lax.all_gather(paired[3], 'dp', axis=0, tiled=True)  125 us
    ppermute x4, waiting for transfers between devices, _take_samples_all(): jax.lax.ppermute(frame_out, axis_tag, perm=tuple(((d, (d - odd) % piece_n...  80.9 us
    all_gather x1, waiting for transfers between devices, collect_trunk(): lax.all_gather(paired[2], 'dp', axis=0, tiled=True)  51.8 us
    all_gather x1, blocking collectives, shards(): lax.all_gather(d_modul, ('dp', 'fsdp'), axis=0, tiled=True)  47.2 us
  transfers between devices with their start and end apart: 15, of which 9 were waited for; matrix products, arithmetic and copies ran while one was open for 9% of the time, Pallas kernels for 0%

profile of v1, /device:TPU:0, one launch (start us, length us, event | category | flops | bytes accessed | tf_op | source)
XLA Modules:
  0.0 1705.1 jit_solution(14160008996555376213)
XLA Ops:
  10.7 5.0 all_gather.30
  23.2 6.7 collective-permute-start
  29.9 14.8 collective-permute-done
  44.8 25.6 %collective-permute-done.1 = bf16[144,3456]{1,0:T(8,128)(2,1)S(1)} collective-permute-done((bf16[144,3456]{1,0:T(8,128)(2,1)S(1)}, bf16[144,3456]{1,0:T(8,128)(2,1)S(1)}, u32[]{:S(2)}, u32[]{:S(2)}) %collective-permute-start.1) | collective-permute-done | bytes 995360 | tf_op jit(solution)/shard_map/ppermute | solution.py:30
  75.0 40.5 %collective-permute-done.2 = bf16[288,3456]{1,0:T(8,128)(2,1)S(1)} collective-permute-done((bf16[288,3456]{1,0:T(8,128)(2,1)S(1)}, bf16[288,3456]{1,0:T(8,128)(2,1)S(1)}, u32[]{:S(2)}, u32[]{:S(2)}) %collective-permute-start.2) | collective-permute-done | bytes 1990688 | tf_op jit(solution)/shard_map/ppermute | solution.py:30
  118.4 10.2 convolution_reduce_fusion
  128.6 215.0 %psum.49 = f32[16]{0:T(128)S(1)} all-reduce(f32[16]{0:T(128)S(1)} %compare_select_fusion.1), channel_id=1, replica_groups=mesh['dp'=16,'fsdp'=2] {'dp','fsdp'}, use_global_device_ids=true, to_apply=%region_6.7 | all-reduce | flops 16 | bytes 128 | tf_op jit(solution)/shard_map/psum | solution.py:112
  355.0 5.4 copy-done.55
  360.4 4.1 fusion.8
  372.1 4.0 fusion.113
  377.5 51.8 %all-gather.11.cloned.1.call-done = bf16[1152,4608]{1,0:T(8,128)(2,1)} async-done(((bf16[72,4608]{1,0:T(8,128)(2,1)}), bf16[1152,4608]{1,0:T(8,128)(2,1)}) %all-gather.11.cloned.1.call-update) | async-done | bytes 10616848 | tf_op jit(solution)/shard_map/all_gather | solution.py:73
  429.3 9.0 convolution_add_fusion
  438.3 125.3 %all-gather.13.cloned.1.call-done = bf16[4608,1152]{1,0:T(8,128)(2,1)} async-done(((bf16[288,1152]{1,0:T(8,128)(2,1)}), bf16[4608,1152]{1,0:T(8,128)(2,1)}) %all-gather.13.cloned.1.call-update) | async-done | bytes 10616848 | tf_op jit(solution)/shard_map/all_gather | solution.py:74
  563.6 10.2 convert_reduce_fusion
  573.9 8.8 fusion.109
  582.8 9.3 fusion.71
  600.3 3.8 convolution_convert_fusion
  606.2 3.7 fusion.82
  609.9 8.5 fusion.52
  618.4 8.6 fusion.58
  631.8 8.2 fusion.97
  641.0 14.1 fusion.100
  655.8 12.0 fusion.106
  668.4 42.1 %all-gather.4 = bf16[32,1,1152]{2,1,0:T(2,128)(2,1)} all-gather(bf16[1,1,1152]{2,1,0:T(2,128)(2,1)S(1)} %copy-done.50), channel_id=1, replica_groups=mesh['dp'=16,'fsdp'=2] {'dp','fsdp'}, dimensions={0}, use_global_device_ids=true | all-gather | bytes 76032 | tf_op jit(solution)/shard_map/all_gather | solution.py:251
  710.5 28.6 %reduce-scatter.33.cloned.1.call-done = f32[72,1152]{1,0:T(8,128)} async-done(((f32[1152,1152]{1,0:T(8,128)}), f32[72,1152]{1,0:T(8,128)}) %reduce-scatter.33.cloned.1.call-update) | async-done | bytes 331792
  741.1 6.7 fusion.69
  749.6 246.3 %reduce-scatter.31.cloned.1.call-done = f32[72,3456]{1,0:T(8,128)} async-done(((f32[1152,3456]{1,0:T(8,128)}), f32[72,3456]{1,0:T(8,128)}) %reduce-scatter.31.cloned.1.call-update) | async-done | bytes 995344
  1006.1 307.7 %reduce-scatter.23.cloned.1.call-done = f32[288,1152]{1,0:T(8,128)} async-done(((f32[4608,1152]{1,0:T(8,128)}), f32[288,1152]{1,0:T(8,128)}) %reduce-scatter.23.cloned.1.call-update) | async-done | bytes 1327120 | tf_op jit(solution)/shard_map/reduce_scatter | solution.py:225
  1316.7 47.2 %all-gather.3 = bf16[32,1,6912]{2,1,0:T(2,128)(2,1)S(1)} all-gather(bf16[1,1,6912]{2,1,0:T(2,128)(2,1)S(1)} %bitcast.189), channel_id=1, replica_groups=mesh['dp'=16,'fsdp'=2] {'dp','fsdp'}, dimensions={0}, use_global_device_ids=true | all-gather | bytes 456192 | tf_op jit(solution)/shard_map/all_gather | solution.py:247
  1363.9 271.6 %reduce-scatter.19.cloned.1.call-done = f32[72,4608]{1,0:T(8,128)} async-done(((f32[1152,4608]{1,0:T(8,128)}), f32[72,4608]{1,0:T(8,128)}) %reduce-scatter.19.cloned.1.call-update) | async-done | bytes 1327120 | tf_op jit(solution)/shard_map/reduce_scatter | solution.py:224
  1639.8 41.1 %all-reduce.2 = (f32[1152]{0:T(1024)}, f32[1152]{0:T(1024)}, f32[1152]{0:T(1024)}, f32[4608]{0:T(1024)}, f32[1152]{0:T(1024)}, /*index=5*/f32[6912]{0:T(1024)}) all-reduce(f32[1152]{0:T(1024)S(1)} %get-tuple-element.19, f32[1152]{0:T(1024)S(1)} %get-tuple-element.18, ...), channel_id=1, replica_groups=mesh['dp'=16,'fsdp'=2] {'dp','fsdp'}, use_global_device_ids=true, to_apply=%region_23.24 | all-reduce | flops 16128 | bytes 115200 | tf_op jit(solution)/shard_map/psum | solution.py:241
  1682.3 8.3 fusion.87
  (245 shorter events, 83.5 us)
Async XLA Ops:
  7.2 364.9 %all-gather.9.cloned.1.call-start = ((), (), s32[]{:S(2)}) async-start(), calls=%async_computation.8 | async-start | bytes 2820096 | tf_op jit(solution)/shard_map/all_gather | solution.py:72
  10.6 418.7 %all-gather.11.cloned.1.call-start = ((), (), s32[]{:S(2)}) async-start(), calls=%async_computation.9 | async-start | bytes 11280384 | tf_op jit(solution)/shard_map/all_gather | solution.py:73
  15.8 547.9 %all-gather.13.cloned.1.call-start = ((), (), s32[]{:S(2)}) async-start(), calls=%async_computation.10 | async-start | bytes 11280384 | tf_op jit(solution)/shard_map/all_gather | solution.py:74
  20.2 718.9 %reduce-scatter.33.cloned.1.call-start = ((), (), s32[]{:S(2)}) async-start(), calls=%async_computation.18 | async-start | bytes 5640192
  23.2 21.4 %collective-permute-start = (bf16[72,3456]{1,0:T(8,128)(2,1)S(1)}, bf16[72,3456]{1,0:T(8,128)(2,1)S(1)}, u32[]{:S(2)}, u32[]{:S(2)}) collective-permute-start(bf16[72,3456]{1,0:T(8,128)(2,1)S(1)} %bitcast.162), channel_id=1, source_target_pairs={{0,30},{2,0},{4,2},{6,4},{8,6},{10,8},{12,10},{14,12},{16,14},{18,... | collective-permute-start | bytes 1493000 | tf_op jit(solution)/shard_map/ppermute | solution.py:30
  44.8 25.6 %collective-permute-start.1 = (bf16[144,3456]{1,0:T(8,128)(2,1)S(1)}, bf16[144,3456]{1,0:T(8,128)(2,1)S(1)}, u32[]{:S(2)}, u32[]{:S(2)}) collective-permute-start(bf16[144,3456]{1,0:T(8,128)(2,1)S(1)} %pad_maximum_fusion.2), channel_id=1, source_target_pairs={{0,28},{2,30},{4,0},{6,2},{8,4},{10,6},{12,8},{14,10},{16,12},{18,... | collective-permute-start | bytes 2985992 | tf_op jit(solution)/shard_map/ppermute | solution.py:30
  70.5 45.0 %collective-permute-start.2 = (bf16[288,3456]{1,0:T(8,128)(2,1)S(1)}, bf16[288,3456]{1,0:T(8,128)(2,1)S(1)}, u32[]{:S(2)}, u32[]{:S(2)}) collective-permute-start(bf16[288,3456]{1,0:T(8,128)(2,1)S(1)} %pad_maximum_fusion.1), channel_id=1, source_target_pairs={{0,24},{2,26},{4,28},{6,30},{8,0},{10,2},{12,4},{14,6},{16,8},{18,... | collective-permute-start | bytes 5971976 | tf_op jit(solution)/shard_map/ppermute | solution.py:30
  117.7 231.4 %collective-permute-start.3 = (bf16[576,3456]{1,0:T(8,128)(2,1)}, bf16[576,3456]{1,0:T(8,128)(2,1)}, u32[]{:S(2)}, u32[]{:S(2)}) collective-permute-start(bf16[576,3456]{1,0:T(8,128)(2,1)} %pad_maximum_fusion), channel_id=1, source_target_pairs={{0,16},{2,18},{4,20},{6,22},{8,24},{10,26},{12,28},{14,30},{16,0},... | collective-permute-start | bytes 11943944 | tf_op jit(solution)/shard_map/ppermute | solution.py:30
  118.4 229.0 %copy-start.58 = (f32[1152]{0:T(1024)S(1)}, f32[1152]{0:T(1024)}, u32[]{:S(2)}) copy-start(f32[1152]{0:T(1024)} %param.25) | copy-start | bytes 13828
  118.4 229.6 %copy-start.1 = (bf16[1,256,1152]{2,1,0:T(8,128)(2,1)S(1)}, bf16[1,256,1152]{2,1,0:T(8,128)(2,1)}, u32[]{:S(2)}) copy-start(bf16[1,256,1152]{2,1,0:T(8,128)(2,1)} %param.17) | copy-start | bytes 1769476
  598.4 397.4 %reduce-scatter.31.cloned.1.call-start = ((), (), s32[]{:S(2)}) async-start(), calls=%async_computation.17 | async-start | bytes 16920576
  639.9 673.8 %reduce-scatter.23.cloned.1.call-start = ((), (), s32[]{:S(2)}) async-start(), calls=%async_computation.13 | async-start | bytes 22560768 | tf_op jit(solution)/shard_map/reduce_scatter | solution.py:225
  655.1 980.4 %reduce-scatter.19.cloned.1.call-start = ((), (), s32[]{:S(2)}) async-start(), calls=%async_computation.11 | async-start | bytes 22560768 | tf_op jit(solution)/shard_map/reduce_scatter | solution.py:224
  667.8 1022.8 %reduce-scatter.27.cloned.1.call-start = ((), (), s32[]{:S(2)}) async-start(), calls=%async_computation.15 | async-start | bytes 442368
  741.0 951.3 %reduce-scatter.25.cloned.1.call-start = ((), (), s32[]{:S(2)}) async-start(), calls=%async_computation.14 | async-start | bytes 1327104
  747.8 254.7 %copy-start.9 = (f32[256,1152]{1,0:T(8,128)S(1)}, f32[256,1152]{1,0:T(8,128)}, u32[]{:S(2)}) copy-start(f32[256,1152]{1,0:T(8,128)} %get-tuple-element.54) | copy-start | bytes 3538948
  747.8 254.7 %copy-start.37 = (f32[256]{0:T(256)S(1)}, f32[256]{0:T(256)}, u32[]{:S(2)}) copy-start(f32[256]{0:T(256)} %copy-done.35) | copy-start | bytes 3076
  1000.2 694.1 %reduce-scatter.29.cloned.1.call-start = ((), (), s32[]{:S(2)}) async-start(), calls=%async_computation.16 | async-start | bytes 1327104
  1006.1 310.5 %copy-start.34 = (bf16[1,6912]{1,0:T(2,128)(2,1)S(1)}, bf16[1,6912]{1,0:T(2,128)(2,1)}, u32[]{:S(2)}) copy-start(bf16[1,6912]{1,0:T(2,128)(2,1)} %constant_dynamic-update-slice_fusion.15) | copy-start | bytes 41476
  1006.1 310.5 %copy-start.54 = (bf16[1152]{0:T(1024)(128)(2,1)S(1)}, bf16[1152]{0:T(1024)(128)(2,1)}, u32[]{:S(2)}) copy-start(bf16[1152]{0:T(1024)(128)(2,1)} %get-tuple-element.16) | copy-start | bytes 6916
  1006.1 310.5 %copy-start.41 = (bf16[1152]{0:T(1024)(128)(2,1)S(1)}, bf16[1152]{0:T(1024)(128)(2,1)}, u32[]{:S(2)}) copy-start(bf16[1152]{0:T(1024)(128)(2,1)} %get-tuple-element.47) | copy-start | bytes 6916
  1006.1 310.5 %copy-start.53 = (bf16[1152]{0:T(1024)(128)(2,1)S(1)}, bf16[1152]{0:T(1024)(128)(2,1)}, u32[]{:S(2)}) copy-start(bf16[1152]{0:T(1024)(128)(2,1)} %get-tuple-element.20) | copy-start | bytes 6916
  1006.1 310.6 %copy-start.52 = (bf16[1152]{0:T(1024)(128)(2,1)S(1)}, bf16[1152]{0:T(1024)(128)(2,1)}, u32[]{:S(2)}) copy-start(bf16[1152]{0:T(1024)(128)(2,1)} %get-tuple-element.46) | copy-start | bytes 6916
  1006.1 310.6 %copy-start.51 = (bf16[1152]{0:T(1024)(128)(2,1)S(1)}, bf16[1152]{0:T(1024)(128)(2,1)}, u32[]{:S(2)}) copy-start(bf16[1152]{0:T(1024)(128)(2,1)} %get-tuple-element.43) | copy-start | bytes 6916
  1316.4 321.7 %copy-start.29 = (bf16[6912]{0:T(1024)(128)(2,1)S(1)}, bf16[6912]{0:T(1024)(128)(2,1)}, u32[]{:S(2)}) copy-start(bf16[6912]{0:T(1024)(128)(2,1)} %custom-call.1) | copy-start | bytes 41476
  1316.4 323.3 %copy-start.42 = (f32[1152]{0:T(1024)S(1)}, f32[1152]{0:T(1024)}, u32[]{:S(2)}) copy-start(f32[1152]{0:T(1024)} %get-tuple-element.38) | copy-start | bytes 13828
  1316.5 323.3 %copy-start.43 = (f32[1152]{0:T(1024)S(1)}, f32[1152]{0:T(1024)}, u32[]{:S(2)}) copy-start(f32[1152]{0:T(1024)} %get-tuple-element.49) | copy-start | bytes 13828
  1316.5 323.3 %copy-start.49 = (f32[4608]{0:T(1024)S(1)}, f32[4608]{0:T(1024)}, u32[]{:S(2)}) copy-start(f32[4608]{0:T(1024)} %get-tuple-element.57) | copy-start | bytes 55300
  1316.5 364.5 %copy-start.19 = (bf16[32,1,1152]{2,1,0:T(2,128)(2,1)S(1)}, bf16[32,1,1152]{2,1,0:T(2,128)(2,1)}, u32[]{:S(2)}) copy-start(bf16[32,1,1152]{2,1,0:T(2,128)(2,1)} %all-gather.4) | copy-start | bytes 221188
  1316.5 380.0 %reduce-scatter.21.cloned.1.call-start = ((), (), s32[]{:S(2)}) async-start(), calls=%async_computation.12 | async-start | bytes 995328 | tf_op jit(solution)/shard_map/reduce_scatter | solution.py:234
  1363.9 318.4 %copy-start.31 = (bf16[1,1152]{1,0:T(2,128)(2,1)S(1)}, bf16[1,1152]{1,0:T(2,128)(2,1)}, u32[]{:S(2)}) copy-start(bf16[1,1152]{1,0:T(2,128)(2,1)} %param.18) | copy-start | bytes 6916
  1363.9 318.4 %copy-start.33 = (f32[1,1152]{1,0:T(1,128)S(1)}, f32[1,1152]{1,0:T(1,128)}, u32[]{:S(2)}) copy-start(f32[1,1152]{1,0:T(1,128)} %copy-done.32) | copy-start | bytes 13828
  (47 other events, 1176.0 us)
Sparse Core Ops, SparseCore 0:
  11.3 216.8 all-gather.8
  231.0 198.2 all-gather.10
  432.7 130.9 all-gather.12
  598.6 140.4 reduce-scatter.32
  744.7 251.0 reduce-scatter.30
  1001.7 312.0 reduce-scatter.22
  1319.8 315.6 reduce-scatter.18
  1638.3 6.8 reduce-scatter.26
  1647.5 9.3 reduce-scatter.24
  1659.0 9.3 reduce-scatter.28
  1671.2 9.2 reduce-scatter.20
